TPU v7x, 128 devices: a whole 4x4x4 slice. The times are simulated.
128 devices in a mesh: rep: 16 (over z, y), shard: 8 (over x, core).
Axes of the slice: x: 4, y: 4, z: 4, core: 2. Of those that a mesh axis runs over, the one named last changes fastest.
Arguments:
- grads: bfloat16 [16, 8, 1024, 1024], P('rep', 'shard'), may hold values from -6 to 6
- master: float32 [8, 256, 1024], P('shard'), may hold values from -4 to 4
- moment_one: float32 [8, 256, 1024], P('shard'), may hold values from -4 to 4
- moment_two: float32 [8, 256, 1024], P('shard'), may hold values from 0.01 to 10
- average: float32 [8, 256, 1024], P('shard'), may hold values from -4 to 4
- tensor_owner: int32 [32], replicated, may hold values from 0 to 7, as said below
- tensor_start: int32 [32], replicated, may hold values from 0 to 1008, as said below
- tensor_rows: int32 [32], replicated, may hold values from 16 to 208, as said below
- tensor_slot: int32 [32], replicated, may hold values from 0 to 240, as said below
Outputs:
- new_params: float32 [1024, 1024], replicated
- master_new: float32 [8, 256, 1024], P('shard')
- moment_one_new: float32 [8, 256, 1024], P('shard')
- moment_two_new: float32 [8, 256, 1024], P('shard')
- average_new: float32 [8, 256, 1024], P('shard')
Inputs may be any that keep to these rules, and one draw needn't show every extreme that they name: `tensor_owner`: every owner holds exactly 4 tensors; one owner's tensors have exactly 256 rows together and no owner's more. `tensor_start`: the tensors cover the window's rows without gaps or intersections. `tensor_rows`: each tensor's rows are a multiple of 16. `tensor_slot`: an owner's tensors fill its buffer rows from 0 upward without gaps or intersections.
All inputs are finite; a program needn't handle non-finite values.
Results may differ from a plain program's by a relative error of at most 0.0003.
Values may be sent and summed in bfloat16 or wider, within the bound.
No kernel may reach another device: no remote copies, remote signals or barrier semaphores. Data moves between devices by JAX's collectives and lax.ppermute only.
A program may use at most 128 MiB of HBM per device.

v0:
```python
import math
import jax
import jax.numpy as jnp
from jax import lax
from jax.sharding import PartitionSpec as P

beta_one = 0.9
beta_two = 0.95
epsilon = 1e-08
learn_rate = 0.01
decay_base = 0.1
average_rate = 0.99
step_count = 10.0
reference_batch = 128.0


def optimizer_step(summed, master, moment_one, moment_two, average, decay_scale):
    moment_one_new = beta_one * moment_one + (1.0 - beta_one) * summed
    moment_two_new = beta_two * moment_two + (1.0 - beta_two) * summed * summed
    corr_one = 1.0 - beta_one**step_count
    corr_two = 1.0 - beta_two**step_count
    update = moment_one_new / corr_one / (jnp.sqrt(moment_two_new / corr_two) + epsilon)
    master_new = master * (1.0 - learn_rate * decay_base * decay_scale) - learn_rate * update
    average_new = average_rate * average + (1.0 - average_rate) * master_new
    return (master_new, moment_one_new, moment_two_new, average_new)


def packed_rows(
    gradient, tensor_owner, tensor_start, tensor_rows, tensor_slot, dest_owner, dest_slot, wire_type
):
    slot_begin = tensor_slot[None, :]
    covered = (
        (dest_owner[:, None] == tensor_owner[None, :])
        & (dest_slot[:, None] >= slot_begin)
        & (dest_slot[:, None] < slot_begin + tensor_rows[None, :])
    )
    offset = tensor_start[None, :] + dest_slot[:, None] - slot_begin
    window_row = jnp.sum(jnp.where(covered, offset, 0), axis=1)
    present = jnp.any(covered, axis=1)
    picked = jnp.take(gradient, window_row, axis=0)
    return jnp.where(present[:, None], picked, jnp.zeros((), wire_type))


def add_sources(received):
    return jnp.sum(received, axis=0, dtype=jnp.float32)


def local(
    grads,
    master,
    moment_one,
    moment_two,
    average,
    tensor_owner,
    tensor_start,
    tensor_rows,
    tensor_slot,
):
    gradient = grads[0, 0]
    owners = lax.axis_size("shard")
    replicas = lax.axis_size("rep")
    capacity = master.shape[1]
    row_width = gradient.shape[1]
    row_total = gradient.shape[0]
    decay_scale = math.sqrt(owners * replicas / reference_batch)
    slot_index = jnp.arange(owners * capacity, dtype=jnp.int32)
    dest_owner = slot_index // capacity
    dest_slot = slot_index % capacity
    window_sum = lax.psum(gradient.astype(jnp.float32), "rep")
    packed = packed_rows(
        window_sum,
        tensor_owner,
        tensor_start,
        tensor_rows,
        tensor_slot,
        dest_owner,
        dest_slot,
        jnp.float32,
    )
    packed = packed.reshape(owners, capacity, row_width)
    summed = add_sources(lax.all_to_all(packed, "shard", split_axis=0, concat_axis=0, tiled=True))
    states = optimizer_step(
        summed, master[0], moment_one[0], moment_two[0], average[0], decay_scale
    )
    updated = states[0]
    row_index = jnp.arange(row_total, dtype=jnp.int32)
    inside = (row_index[:, None] >= tensor_start[None, :]) & (
        row_index[:, None] < (tensor_start + tensor_rows)[None, :]
    )
    target = tensor_owner * capacity + tensor_slot - tensor_start
    destination = jnp.sum(jnp.where(inside, target[None, :] + row_index[:, None], 0), axis=1)
    piece = lax.all_gather(updated, "shard", axis=0, tiled=True)
    within = (destination >= 0) & (destination < piece.shape[0])
    picked = jnp.take(piece, jnp.clip(destination, 0, piece.shape[0] - 1), axis=0)
    new_params = jnp.where(within[:, None], picked, jnp.zeros((row_total, row_width), jnp.float32))
    return (new_params, states[0][None], states[1][None], states[2][None], states[3][None])


def solution(mesh):
    in_specs = (
        P("rep", "shard", None, None),
        P("shard", None, None),
        P("shard", None, None),
        P("shard", None, None),
        P("shard", None, None),
        P(),
        P(),
        P(),
        P(),
    )
    out_specs = (
        P(),
        P("shard", None, None),
        P("shard", None, None),
        P("shard", None, None),
        P("shard", None, None),
    )
    return jax.shard_map(local, mesh=mesh, in_specs=in_specs, out_specs=out_specs, check_vma=False)
```

profile of v0, /device:TPU:1, one launch (start us, length us, event | category | flops | bytes accessed | tf_op | source)
XLA Modules:
  0.0 313.1 jit_solution(11101088858374454357)
XLA Ops:
  7.2 0.0 copy-start.3
  7.2 0.0 copy-start.4
  7.2 0.0 copy-start.5
  7.2 0.0 copy-start.2
  7.2 0.0 all-reduce.2.cloned.1.call-start
  7.3 4.1 %bitcast_convert_fusion = f32[1024,1024]{1,0:T(8,128)} fusion(bf16[1,1,1024,1024]{3,2,1,0:T(8,128)(2,1)} %param.9), kind=kLoop, calls=%fused_computation.4 | loop fusion | flops 1048576 | bytes 6291456 | tf_op jit(solution)/shard_map/convert_element_type | solution.py:69
  11.3 0.0 all-reduce.2.cloned.1.call-update
  11.3 0.0 all-gather.2.cloned.1.call-start
  11.4 0.0 copy-done.3
  11.4 0.0 copy-done.4
  11.4 0.0 copy-done.5
  11.4 0.0 copy-done.2
  11.5 0.2 select_reduce_fusion
  11.6 0.2 fusion.18
  11.9 106.7 %all-reduce.2.cloned.1.call-done = f32[1024,1024]{1,0:T(8,128)} async-done(((f32[1024,1024]{1,0:T(8,128)}), f32[1024,1024]{1,0:T(8,128)}) %all-reduce.2.cloned.1.call-update) | async-done | bytes 4194320 | tf_op jit(solution)/shard_map/psum | solution.py:69
  118.6 13.9 %gather_fusion = f32[2048,1024]{1,0:T(8,128)} fusion(f32[1024,1024]{1,0:T(8,128)} %all-reduce.2.cloned.1.call-done, s32[2048]{0:T(1024)S(1)} %broadcast_clamp_fusion), kind=kCustom, calls=%fused_computation | custom fusion | bytes 16785408 | tf_op jit(solution)/shard_map/jit(_take)/gather | solution.py:40
  132.4 4.0 %select_select_fusion = f32[8,256,1024]{2,1,0:T(8,128)S(1)} fusion(f32[8,256,1024]{2,1,0:T(8,128)} %bitcast.25, pred[8,256]{1,0:T(8,128)(4,1)S(1)} %compare_and_fusion.1, pred[8,256]{1,0:T(8,128)(4,1)S(1)} %broadcast_in_dim.76), kind=kLoop, calls=%fused_computation.2 | loop fusion | flops 4194304 | bytes 16781312 | tf_op jit(solution)/shard_map/jit(_where)/select_n | solution.py:41
  136.4 100.0 %all_to_all.5 = f32[8,256,1024]{2,1,0:T(8,128)} all-to-all(f32[8,256,1024]{2,1,0:T(8,128)S(1)} %select_select_fusion), channel_id=1, replica_groups=mesh['rep'=16,'shard'=8] {'shard'}, dimensions={0} | all-to-all | bytes 16777216 | tf_op jit(solution)/shard_map/all_to_all | solution.py:81
  236.4 0.0 copy-start
  236.4 0.0 copy-start.1
  236.4 4.5 %reduce_sum.37 = f32[256,1024]{1,0:T(8,128)S(1)} reduce(f32[8,256,1024]{2,1,0:T(8,128)} %all_to_all.5, f32[]{:T(128)} %constant.83.clone.1), dimensions={0}, to_apply=%region_4.5 | reduce | flops 1835008 | bytes 9437188 | tf_op jit(solution)/shard_map/reduce_sum | solution.py:45
  241.0 0.0 copy-done
  241.0 0.0 copy-done.1
  241.0 3.0 fusion.6
  243.9 0.0 all-gather.2.cloned.1.call-update
  244.0 0.1 select_reduce_fusion.1
  244.1 4.2 %multiply_add_fusion = (f32[1,256,1024]{2,1,0:T(8,128)}, f32[1,256,1024]{2,1,0:T(8,128)}, f32[1,256,1024]{2,1,0:T(8,128)}, f32[1,256,1024]{2,1,0:T(8,128)}) fusion(f32[1,256,1024]{2,1,0:T(8,128)} %param.13, f32[1,256,1024]{2,1,0:T(8,128)} %param.10, f32[256,1024]{1,0:T(8,128)S(1)} %reduce_sum.37, f32[1,256,1024]{2,1,0:T(8,128)S(1)} %copy-done.1, ...), kind=kLoop, calls=%fused_computation.19 | loop fusion | flops 4456448 | bytes 9437184 | tf_op jit(solution)/shard_map/add | solution.py:24
  248.4 44.1 %all-gather.2.cloned.1.call-done = f32[2048,1024]{1,0:T(8,128)} async-done(((f32[256,1024]{1,0:T(8,128)}), f32[2048,1024]{1,0:T(8,128)}) %all-gather.2.cloned.1.call-update) | async-done | bytes 8388624 | tf_op jit(solution)/shard_map/all_gather | solution.py:92
  292.4 9.7 %gather_fusion.1 = f32[1024,1024]{1,0:T(8,128)} fusion(f32[2048,1024]{1,0:T(8,128)} %all-gather.2.cloned.1.call-done, s32[1024]{0:T(1024)S(1)} %broadcast_clamp_fusion.1), kind=kCustom, calls=%fused_computation.1 | custom fusion | bytes 8392704 | tf_op jit(solution)/shard_map/jit(_take)/gather | solution.py:94
  302.1 4.2 %select_select_fusion.1 = f32[1024,1024]{1,0:T(8,128)} fusion(f32[1024,1024]{1,0:T(8,128)} %gather_fusion.1, pred[1024]{0:T(1024)(128)(4,1)S(1)} %get-tuple-element.10, pred[1024]{0:T(1024)(128)(4,1)S(1)} %get-tuple-element.9), kind=kLoop, calls=%fused_computation.3 | loop fusion | flops 2097152 | bytes 8390656 | tf_op jit(solution)/shard_map/jit(_where)/select_n | solution.py:95
  (11 shorter events, 0.1 us)
Async XLA Ops:
  7.2 4.2 %copy-start.3 = (s32[32]{0:T(128)S(1)}, s32[32]{0:T(128)}, u32[]{:S(2)}) copy-start(s32[32]{0:T(128)} %param.14) | copy-start | bytes 388
  7.2 4.2 %copy-start.4 = (s32[32]{0:T(128)S(1)}, s32[32]{0:T(128)}, u32[]{:S(2)}) copy-start(s32[32]{0:T(128)} %param.15) | copy-start | bytes 388
  7.2 4.2 %copy-start.5 = (s32[32]{0:T(128)S(1)}, s32[32]{0:T(128)}, u32[]{:S(2)}) copy-start(s32[32]{0:T(128)} %param.16) | copy-start | bytes 388
  7.2 4.2 %copy-start.2 = (s32[32]{0:T(128)S(1)}, s32[32]{0:T(128)}, u32[]{:S(2)}) copy-start(s32[32]{0:T(128)} %param.17) | copy-start | bytes 388
  7.2 111.4 %all-reduce.2.cloned.1.call-start = ((), (), s32[]{:S(2)}) async-start(), calls=%async_computation.1 | async-start | bytes 8388608 | tf_op jit(solution)/shard_map/psum | solution.py:69
  11.3 281.1 %all-gather.2.cloned.1.call-start = ((), (), s32[]{:S(2)}) async-start(), calls=%async_computation.2 | async-start | bytes 9437184 | tf_op jit(solution)/shard_map/all_gather | solution.py:92
  236.4 4.5 %copy-start = (f32[1,256,1024]{2,1,0:T(8,128)S(1)}, f32[1,256,1024]{2,1,0:T(8,128)}, u32[]{:S(2)}) copy-start(f32[1,256,1024]{2,1,0:T(8,128)} %param.12) | copy-start | bytes 3145732
  236.4 4.5 %copy-start.1 = (f32[1,256,1024]{2,1,0:T(8,128)S(1)}, f32[1,256,1024]{2,1,0:T(8,128)}, u32[]{:S(2)}) copy-start(f32[1,256,1024]{2,1,0:T(8,128)} %param.11) | copy-start | bytes 3145732
Sparse Core Ops, SparseCore 0:
  12.0 106.5 all-reduce.1
  244.1 48.2 all-gather.1
where the time goes:
time: 313 us
  waiting for transfers between devices  151 us (48%)
  blocking collectives  100 us (32%)
  other arithmetic  24.4 us (8%)
  local copies, waits for them, and re-layouts  23.6 us (8%)
  between operations  14.2 us (5%)
    psum x1, waiting for transfers between devices, local(): window_sum = lax.psum(gradient.astype(jnp.float32), 'rep')  107 us
    all_to_all x1, blocking collectives, local(): lax.all_to_all(packed, 'shard', split_axis=0, concat_axis=0, tiled=True)  100 us
    all_gather x1, waiting for transfers between devices, local(): piece = lax.all_gather(updated, 'shard', axis=0, tiled=True)  44.1 us
    gather x1, local copies, waits for them, and re-layouts, packed_rows(): picked = jnp.take(gradient, window_row, axis=0)  13.9 us
    gather x1, local copies, waits for them, and re-layouts, local(): jnp.take(piece, jnp.clip(destination, 0, piece.shape[0] - 1), axis=0)  9.71 us
  transfers between devices with their start and end apart: 2, of which 2 were waited for; matrix products, arithmetic and copies ran while one was open for 2% of the time, Pallas kernels for 0%

commit v1 on v0

--- a/solution.py
+++ b/solution.py
@@ -66,7 +66,7 @@
     slot_index = jnp.arange(owners * capacity, dtype=jnp.int32)
     dest_owner = slot_index // capacity
     dest_slot = slot_index % capacity
-    window_sum = lax.psum(gradient.astype(jnp.float32), "rep")
+    window_sum = jnp.sum(lax.all_gather(gradient.astype(jnp.float32), "rep"), axis=0)
     packed = packed_rows(
         window_sum,
         tensor_owner,

time: 313 us -> 601 us (1.92)
  waiting for transfers between devices: 151 us -> 416 us
  other arithmetic: 24.4 us -> 47.4 us
    all_gather x0 -> x1, waiting for transfers between devices: none -> 372 us  [local(): lax.all_gather(gradient.astype(jnp.float32), 'rep')]
    psum x1 -> x0, waiting for transfers between devices: 107 us -> none  [local(): window_sum = lax.psum(gradient.astype(jnp.float32), 'rep')]
    reduce_sum x0 -> x1, other arithmetic: none -> 23 us  [local(): jnp.sum(lax.all_gather(gradient.astype(jnp.float32), 'rep'), axis=0)]
  transfers between devices with their start and end apart: 2 -> 2, of which waited for: 2 -> 2; matrix products, arithmetic and copies ran while one was open for 2% -> 1% of each run, Pallas kernels for 0% -> 0%
where the time goes in v1:
time: 601 us
  waiting for transfers between devices  416 us (69%)
  blocking collectives  99.7 us (17%)
  other arithmetic  47.4 us (8%)
  local copies, waits for them, and re-layouts  23.6 us (4%)
  between operations  14.2 us (2%)
    all_gather x1, waiting for transfers between devices, local(): lax.all_gather(gradient.astype(jnp.float32), 'rep')  372 us
    all_to_all x1, blocking collectives, local(): lax.all_to_all(packed, 'shard', split_axis=0, concat_axis=0, tiled=True)  99.7 us
    all_gather x1, waiting for transfers between devices, local(): piece = lax.all_gather(updated, 'shard', axis=0, tiled=True)  44 us
    reduce_sum x1, other arithmetic, local(): jnp.sum(lax.all_gather(gradient.astype(jnp.float32), 'rep'), axis=0)  23 us
    gather x1, local copies, waits for them, and re-layouts, packed_rows(): picked = jnp.take(gradient, window_row, axis=0)  13.9 us
  transfers between devices with their start and end apart: 2, of which 2 were waited for; matrix products, arithmetic and copies ran while one was open for 1% of the time, Pallas kernels for 0%

profile of v1, /device:TPU:1, one launch (start us, length us, event | category | flops | bytes accessed | tf_op | source)
XLA Modules:
  0.0 600.7 jit_solution(15559990815617945236)
XLA Ops:
  7.2 0.0 copy-start.4
  7.2 0.0 copy-start.2
  7.2 0.0 copy-start.5
  7.2 0.0 copy-start.3
  7.2 0.0 all-gather.6.cloned.1.call-start
  7.3 4.1 convert_element_type.15
  11.3 0.0 all-gather.6.cloned.1.call-update
  11.3 0.0 all-gather.4.cloned.1.call-start
  11.4 0.0 copy-done.4
  11.4 0.0 copy-done.2
  11.4 0.0 copy-done.5
  11.4 0.0 copy-done.3
  11.5 0.2 select_reduce_fusion
  11.6 0.2 fusion.18
  11.9 371.6 %all-gather.6.cloned.1.call-done = f32[16,1,1024,1024]{3,2,1,0:T(8,128)} async-done(((f32[1,1,1024,1024]{3,2,1,0:T(8,128)}), f32[16,1,1024,1024]{3,2,1,0:T(8,128)}) %all-gather.6.cloned.1.call-update) | async-done | bytes 67108880 | tf_op jit(solution)/shard_map/all_gather | solution.py:69
  383.5 23.0 %reduce_sum.45 = f32[1024,1024]{1,0:T(8,128)} reduce(f32[16,1,1024,1024]{3,2,1,0:T(8,128)} %all-gather.6.cloned.1.call-done, f32[]{:T(128)} %constant.82.clone.1), dimensions={0,1}, to_apply=%region_3.4 | reduce | flops 15728640 | bytes 71303168 | tf_op jit(solution)/shard_map/reduce_sum | solution.py:69
  406.5 13.9 %gather_fusion = f32[2048,1024]{1,0:T(8,128)} fusion(f32[1024,1024]{1,0:T(8,128)} %reduce_sum.45, s32[2048]{0:T(1024)S(1)} %broadcast_clamp_fusion), kind=kCustom, calls=%fused_computation | custom fusion | bytes 16785408 | tf_op jit(solution)/shard_map/jit(_take)/gather | solution.py:40
  420.3 4.0 select_select_fusion
  424.3 99.7 %all_to_all.5 = f32[8,256,1024]{2,1,0:T(8,128)} all-to-all(f32[8,256,1024]{2,1,0:T(8,128)S(1)} %select_select_fusion), channel_id=1, replica_groups=mesh['rep'=16,'shard'=8] {'shard'}, dimensions={0} | all-to-all | bytes 16777216 | tf_op jit(solution)/shard_map/all_to_all | solution.py:81
  524.0 0.0 copy-start
  524.0 0.0 copy-start.1
  524.1 4.5 reduce_sum.47
  528.6 0.0 copy-done
  528.6 0.0 copy-done.1
  528.6 3.0 fusion.6
  531.6 0.0 all-gather.4.cloned.1.call-update
  531.6 0.1 select_reduce_fusion.1
  531.7 4.2 multiply_add_fusion
  536.0 44.0 %all-gather.4.cloned.1.call-done = f32[2048,1024]{1,0:T(8,128)} async-done(((f32[256,1024]{1,0:T(8,128)}), f32[2048,1024]{1,0:T(8,128)}) %all-gather.4.cloned.1.call-update) | async-done | bytes 8388624 | tf_op jit(solution)/shard_map/all_gather | solution.py:92
  580.0 9.7 %gather_fusion.1 = f32[1024,1024]{1,0:T(8,128)} fusion(f32[2048,1024]{1,0:T(8,128)} %all-gather.4.cloned.1.call-done, s32[1024]{0:T(1024)S(1)} %broadcast_clamp_fusion.1), kind=kCustom, calls=%fused_computation.1 | custom fusion | bytes 8392704 | tf_op jit(solution)/shard_map/jit(_take)/gather | solution.py:94
  589.7 4.2 select_select_fusion.1
  (11 shorter events, 0.1 us)
Async XLA Ops:
  7.2 4.2 copy-start.4
  7.2 4.2 copy-start.2
  7.2 4.2 copy-start.5
  7.2 4.2 copy-start.3
  7.2 376.3 %all-gather.6.cloned.1.call-start = ((), (), s32[]{:S(2)}) async-start(), calls=%async_computation.2 | async-start | bytes 71303168 | tf_op jit(solution)/shard_map/all_gather | solution.py:69
  11.3 568.7 %all-gather.4.cloned.1.call-start = ((), (), s32[]{:S(2)}) async-start(), calls=%async_computation.1 | async-start | bytes 9437184 | tf_op jit(solution)/shard_map/all_gather | solution.py:92
  524.0 4.5 copy-start
  524.0 4.5 copy-start.1
Sparse Core Ops, SparseCore 0:
  11.5 371.9 all-gather.5
  531.7 48.2 all-gather.3

commit v2 on v0

--- a/solution.py
+++ b/solution.py
@@ -89,7 +89,9 @@
     )
     target = tensor_owner * capacity + tensor_slot - tensor_start
     destination = jnp.sum(jnp.where(inside, target[None, :] + row_index[:, None], 0), axis=1)
-    piece = lax.all_gather(updated, "shard", axis=0, tiled=True)
+    piece = jnp.concatenate(
+        lax.all_to_all(jnp.stack([updated] * lax.axis_size("shard")), "shard", 0, 0), axis=0
+    )
     within = (destination >= 0) & (destination < piece.shape[0])
     picked = jnp.take(piece, jnp.clip(destination, 0, piece.shape[0] - 1), axis=0)
     new_params = jnp.where(within[:, None], picked, jnp.zeros((row_total, row_width), jnp.float32))

time: 313 us -> 370 us (1.18)
  waiting for transfers between devices: 151 us -> 200 us
  starting transfers between devices: 0.08 us -> 5.91 us
  local copies, waits for them, and re-layouts: 23.6 us -> 28 us
    all_to_all x0 -> x1, waiting for transfers between devices: none -> 93.7 us  [local(): lax.all_to_all(jnp.stack([updated] * lax.axis_size('shard')), 'shard', 0, 0)]
    all_gather x1 -> x0, waiting for transfers between devices: 44.1 us -> none  [local(): piece = lax.all_gather(updated, 'shard', axis=0, tiled=True)]
    all_to_all x0 -> x1, starting transfers between devices: none -> 5.87 us  [local(): lax.all_to_all(jnp.stack([updated] * lax.axis_size('shard')), 'shard', 0, 0)]
    another operation x0 -> x1, local copies, waits for them, and re-layouts: none -> 4.27 us  [local(): jnp.stack([updated] * lax.axis_size('shard'))]
  transfers between devices with their start and end apart: 2 -> 2, of which waited for: 2 -> 2; matrix products, arithmetic and copies ran while one was open for 2% -> 0% of each run, Pallas kernels for 0% -> 0%
where the time goes in v2:
time: 370 us
  waiting for transfers between devices  200 us (54%)
  blocking collectives  100 us (27%)
  local copies, waits for them, and re-layouts  28 us (8%)
  other arithmetic  21.4 us (6%)
  between operations  14.2 us (4%)
  starting transfers between devices  5.91 us (2%)
    psum x1, waiting for transfers between devices, local(): window_sum = lax.psum(gradient.astype(jnp.float32), 'rep')  107 us
    all_to_all x1, blocking collectives, local(): lax.all_to_all(packed, 'shard', split_axis=0, concat_axis=0, tiled=True)  100 us
    all_to_all x1, waiting for transfers between devices, local(): lax.all_to_all(jnp.stack([updated] * lax.axis_size('shard')), 'shard', 0, 0)  93.7 us
    gather x1, local copies, waits for them, and re-layouts, packed_rows(): picked = jnp.take(gradient, window_row, axis=0)  13.9 us
    gather x1, local copies, waits for them, and re-layouts, local(): jnp.take(piece, jnp.clip(destination, 0, piece.shape[0] - 1), axis=0)  9.72 us
  transfers between devices with their start and end apart: 2, of which 2 were waited for; matrix products, arithmetic and copies ran while one was open for 0% of the time, Pallas kernels for 0%

profile of v2, /device:TPU:1, one launch (start us, length us, event | category | flops | bytes accessed | tf_op | source)
XLA Modules:
  0.0 369.9 jit_solution(15231252417421657724)
XLA Ops:
  7.2 0.0 copy-start.3
  7.2 0.0 copy-start.4
  7.2 0.0 copy-start.5
  7.2 0.0 copy-start.2
  7.2 0.0 all-reduce.2.cloned.1.call-start
  7.3 4.1 %bitcast_convert_fusion = f32[1024,1024]{1,0:T(8,128)} fusion(bf16[1,1,1024,1024]{3,2,1,0:T(8,128)(2,1)} %param.9), kind=kLoop, calls=%fused_computation.4 | loop fusion | flops 1048576 | bytes 6291456 | tf_op jit(solution)/shard_map/convert_element_type | solution.py:69
  11.3 0.0 all-reduce.2.cloned.1.call-update
  11.4 0.0 copy-done.3
  11.4 0.0 copy-done.4
  11.4 0.0 copy-done.5
  11.4 0.0 copy-done.2
  11.4 0.2 select_reduce_fusion
  11.6 0.2 fusion.10
  11.9 106.7 %all-reduce.2.cloned.1.call-done = f32[1024,1024]{1,0:T(8,128)} async-done(((f32[1024,1024]{1,0:T(8,128)}), f32[1024,1024]{1,0:T(8,128)}) %all-reduce.2.cloned.1.call-update) | async-done | bytes 4194320 | tf_op jit(solution)/shard_map/psum | solution.py:69
  118.6 13.9 %gather_fusion = f32[2048,1024]{1,0:T(8,128)} fusion(f32[1024,1024]{1,0:T(8,128)} %all-reduce.2.cloned.1.call-done, s32[2048]{0:T(1024)S(1)} %broadcast_clamp_fusion), kind=kCustom, calls=%fused_computation | custom fusion | bytes 16785408 | tf_op jit(solution)/shard_map/jit(_take)/gather | solution.py:40
  132.5 4.0 %select_select_fusion = f32[8,256,1024]{2,1,0:T(8,128)S(1)} fusion(f32[8,256,1024]{2,1,0:T(8,128)} %bitcast.17, pred[8,256]{1,0:T(8,128)(4,1)S(1)} %compare_and_fusion.1, pred[8,256]{1,0:T(8,128)(4,1)S(1)} %broadcast_in_dim.76), kind=kLoop, calls=%fused_computation.2 | loop fusion | flops 4194304 | bytes 16781312 | tf_op jit(solution)/shard_map/jit(_where)/select_n | solution.py:41
  136.5 100.0 %all_to_all.10 = f32[8,256,1024]{2,1,0:T(8,128)} all-to-all(f32[8,256,1024]{2,1,0:T(8,128)S(1)} %select_select_fusion), channel_id=1, replica_groups=mesh['rep'=16,'shard'=8] {'shard'}, dimensions={0} | all-to-all | bytes 16777216 | tf_op jit(solution)/shard_map/all_to_all | solution.py:81
  236.5 0.0 copy-start.1
  236.5 4.5 %reduce_sum.37 = f32[256,1024]{1,0:T(8,128)S(1)} reduce(f32[8,256,1024]{2,1,0:T(8,128)} %all_to_all.10, f32[]{:T(128)} %constant.83.clone.1), dimensions={0}, to_apply=%region_4.5 | reduce | flops 1835008 | bytes 9437188 | tf_op jit(solution)/shard_map/reduce_sum | solution.py:45
  241.0 0.0 copy-done.1
  241.0 4.2 %multiply_add_fusion = (f32[1,256,1024]{2,1,0:T(8,128)}, f32[1,256,1024]{2,1,0:T(8,128)S(1)}, f32[1,256,1024]{2,1,0:T(8,128)}, f32[1,256,1024]{2,1,0:T(8,128)}) fusion(f32[1,256,1024]{2,1,0:T(8,128)S(1)} %copy-done.1, f32[1,256,1024]{2,1,0:T(8,128)} %param.10, f32[256,1024]{1,0:T(8,128)S(1)} %reduce_sum.37, f32[1,256,1024]{2,1,0:T(8,128)} %param.11, ...), kind=kLoop, calls=%fused_computation.9 | loop fusion | flops 4456448 | bytes 9437184 | tf_op jit(solution)/shard_map/add | solution.py:24
  245.2 0.0 copy-start
  245.2 4.3 %stack.5 = f32[8,256,1024]{2,1,0:T(8,128)} broadcast(f32[256,1024]{1,0:T(8,128)S(1)} %bitcast.18), dimensions={1,2} | broadcast | bytes 9437184 | tf_op jit(solution)/shard_map/stack | solution.py:93
  249.4 0.0 copy-done
  249.4 5.9 %all-to-all-start.1 = ((f32[8,256,1024]{2,1,0:T(8,128)}), f32[8,256,1024]{2,1,0:T(8,128)}, u32[]{:S(2)}, u32[]{:S(2)}) async-start(f32[8,256,1024]{2,1,0:T(8,128)} %stack.5), calls=%async_computation.1 | async-start | bytes 16777216 | tf_op jit(solution)/shard_map/all_to_all | solution.py:93
  255.3 0.1 select_reduce_fusion.1
  255.5 93.7 %all-to-all-done.1 = f32[8,256,1024]{2,1,0:T(8,128)} async-done(((f32[8,256,1024]{2,1,0:T(8,128)}), f32[8,256,1024]{2,1,0:T(8,128)}, u32[]{:S(2)}, u32[]{:S(2)}) %all-to-all-start.1) | async-done | bytes 8388640 | tf_op jit(solution)/shard_map/all_to_all | solution.py:93
  349.2 9.7 %gather_fusion.1 = f32[1024,1024]{1,0:T(8,128)} fusion(f32[2048,1024]{1,0:T(8,128)} %bitcast.6, s32[1024]{0:T(1024)S(1)} %broadcast_clamp_fusion.1), kind=kCustom, calls=%fused_computation.1 | custom fusion | bytes 8392704 | tf_op jit(solution)/shard_map/jit(_take)/gather | solution.py:96
  358.9 4.2 %select_select_fusion.1 = f32[1024,1024]{1,0:T(8,128)} fusion(f32[1024,1024]{1,0:T(8,128)} %gather_fusion.1, pred[1024]{0:T(1024)(128)(4,1)S(1)} %get-tuple-element.10, pred[1024]{0:T(1024)(128)(4,1)S(1)} %get-tuple-element.9), kind=kLoop, calls=%fused_computation.3 | loop fusion | flops 2097152 | bytes 8390656 | tf_op jit(solution)/shard_map/jit(_where)/select_n | solution.py:97
  (11 shorter events, 0.1 us)
Async XLA Ops:
  7.2 4.2 %copy-start.3 = (s32[32]{0:T(128)S(1)}, s32[32]{0:T(128)}, u32[]{:S(2)}) copy-start(s32[32]{0:T(128)} %param.14) | copy-start | bytes 388
  7.2 4.2 %copy-start.4 = (s32[32]{0:T(128)S(1)}, s32[32]{0:T(128)}, u32[]{:S(2)}) copy-start(s32[32]{0:T(128)} %param.15) | copy-start | bytes 388
  7.2 4.2 %copy-start.5 = (s32[32]{0:T(128)S(1)}, s32[32]{0:T(128)}, u32[]{:S(2)}) copy-start(s32[32]{0:T(128)} %param.16) | copy-start | bytes 388
  7.2 4.2 %copy-start.2 = (s32[32]{0:T(128)S(1)}, s32[32]{0:T(128)}, u32[]{:S(2)}) copy-start(s32[32]{0:T(128)} %param.17) | copy-start | bytes 388
  7.2 111.4 %all-reduce.2.cloned.1.call-start = ((), (), s32[]{:S(2)}) async-start(), calls=%async_computation.2 | async-start | bytes 8388608 | tf_op jit(solution)/shard_map/psum | solution.py:69
  236.5 4.5 %copy-start.1 = (f32[1,256,1024]{2,1,0:T(8,128)S(1)}, f32[1,256,1024]{2,1,0:T(8,128)}, u32[]{:S(2)}) copy-start(f32[1,256,1024]{2,1,0:T(8,128)} %param.13) | copy-start | bytes 3145732
  245.2 4.3 %copy-start = (f32[1,256,1024]{2,1,0:T(8,128)}, f32[1,256,1024]{2,1,0:T(8,128)S(1)}, u32[]{:S(2)}) copy-start(f32[1,256,1024]{2,1,0:T(8,128)S(1)} %get-tuple-element.6) | copy-start | bytes 3145732
  249.4 99.7 %all-to-all-start.1 = ((f32[8,256,1024]{2,1,0:T(8,128)}), f32[8,256,1024]{2,1,0:T(8,128)}, u32[]{:S(2)}, u32[]{:S(2)}) async-start(f32[8,256,1024]{2,1,0:T(8,128)} %stack.5), calls=%async_computation.1 | async-start | bytes 16777216 | tf_op jit(solution)/shard_map/all_to_all | solution.py:93
Sparse Core Ops, SparseCore 0:
  12.0 106.5 all-reduce.1
